TPU v7x, 32 devices: a whole 2x2x4 slice. The times are simulated.
32 devices in a mesh: groups: 2 (over y), tok: 4 (over z), lay: 2 (over x), head: 2 (over core).
Axes of the slice: x: 2, y: 2, z: 4, core: 2. Of those that a mesh axis runs over, the one named last changes fastest.
Arguments:
- keys: float32 [2, 4096, 1024], P('lay', ('groups', 'tok'), 'head'), parts along dimension 1, may hold values from -80 to 80, as said below
- values: float32 [2, 4096, 1024], P('lay', ('groups', 'tok'), 'head'), parts along dimension 1, may hold values from -24 to 24
- queries: float32 [2, 32, 8192], P('lay', 'groups', 'head'), parts along dimension 1, may hold values from -620 to 620, as said below
- start_block: float32 [4096, 256], P(('groups', 'tok')), parts along dimension 0, may hold values from -6 to 6
- lengths: int32 [32], P('groups'), parts along dimension 0, may hold values from 1 to 2048, as said below
Outputs:
- attended: float32 [2, 32, 2, 4096], P('lay', 'groups', 'head', 'tok'), parts along dimension 1
There are 2 independent parts, one for each index of `groups`. A program takes and returns all parts, laid end to end along the dimension named above; each array names one. Nothing has to cross between parts.
Inputs may be any that keep to these rules, and one draw needn't show every extreme that they name: keys lie within this range. queries lie within this range. `lengths`: the longest row covers all 2048 tokens.
All inputs are finite; a program needn't handle non-finite values.
Results may differ from a plain program's by a relative error of at most 0.0003.
Values sent between devices are 32-bit elements; how exact they have to be, the bound alone decides.
No kernel may reach another device: no remote copies, remote signals or barrier semaphores. Data moves between devices by JAX's collectives and lax.ppermute only.
A program may use at most 64 MiB of HBM per device.

v0:
```python
import math
import jax
import jax.numpy as jnp
from jax import lax
from jax.sharding import PartitionSpec as P

KVH = 8
HD = 128
QH = 64
ITERS = 2
NEG = -1e30


def joined(part, axis, combine):
    gathered = jax.tree.map(lambda a: lax.all_gather(a, axis), part)

    def take(source):
        return jax.tree.map(lambda a: lax.dynamic_index_in_dim(a, source, 0, False), gathered)

    return lax.fori_loop(
        1, lax.axis_size(axis), lambda source, state: combine(state, take(source)), take(0)
    )


def gram_of(block):
    return jnp.dot(
        block.T, block, precision=lax.Precision.HIGHEST, preferred_element_type=jnp.float32
    )


def right_solve(lower, matrix):
    return lax.linalg.triangular_solve(lower, matrix, left_side=False, lower=True, transpose_a=True)


def project(keys, basis):
    return jnp.einsum("lsc,sr->lcr", keys, basis, precision=lax.Precision.HIGHEST)


def mix_block(keys, coef):
    partial_block = jnp.einsum("lsc,lcr->sr", keys, coef, precision=lax.Precision.HIGHEST)
    return lax.psum(partial_block, ("lay", "head"))


def combine(first, second):
    top = jnp.maximum(first[0], second[0])
    scale_one = jnp.exp(first[0] - top)
    scale_two = jnp.exp(second[0] - top)
    total = first[1] * scale_one + second[1] * scale_two
    summed = first[2] * scale_one[..., None] + second[2] * scale_two[..., None]
    return (top, total, summed)


def body(keys, values, queries, start_block, lengths):
    highest = lax.Precision.HIGHEST
    lay_dev, tok_dev, kv_dev = keys.shape
    rank = start_block.shape[1]
    rows = queries.shape[1]
    local_heads = queries.shape[2] // HD
    group = QH // KVH
    kv_local = kv_dev // HD

    def finish(block):
        gram, proj = lax.psum((gram_of(block), project(keys, block)), "tok")
        lower = jnp.linalg.cholesky(gram)
        coef_new = right_solve(lower, proj.reshape(-1, rank)).reshape(proj.shape)
        return (right_solve(lower, block), coef_new)

    basis, coef = finish(start_block)
    for step in range(ITERS):
        basis, coef = finish(mix_block(keys, coef))
    quer = queries.reshape(lay_dev, rows, kv_local, group, HD)
    factor = coef.reshape(lay_dev, kv_local, HD, rank)
    reduced = jnp.einsum("lbgid,lgdr->lgibr", quer, factor, precision=highest) / math.sqrt(HD)
    reduced = reduced.reshape(lay_dev, kv_local, group * rows, rank)
    scores = jnp.einsum("tr,lgxr->tlgx", basis, reduced, precision=highest)
    position = lax.axis_index("tok") * tok_dev + jnp.arange(tok_dev, dtype=jnp.int32)
    valid = position[:, None] < lengths[None, :]
    valid = jnp.tile(valid, (1, group))[:, None, None, :]
    peak = jnp.max(jnp.where(valid, scores, NEG), axis=0)
    weight = jnp.where(valid, jnp.exp(scores - peak[None]), 0.0)
    total = jnp.sum(weight, axis=0)
    vals = values.reshape(lay_dev, tok_dev, kv_local, HD)
    summed = jnp.einsum("tlgx,ltgd->lgxd", weight, vals, precision=highest)
    peak = peak.reshape(lay_dev, local_heads, rows)
    total = total.reshape(lay_dev, local_heads, rows)
    summed = summed.reshape(lay_dev, local_heads, rows, HD)
    share = local_heads // lax.axis_size("tok")
    top, whole_total, whole_sum = joined((peak, total, summed), "tok", combine)
    result = whole_sum / whole_total[..., None]
    result = lax.dynamic_slice_in_dim(result, lax.axis_index("tok") * share, share, 1)
    result = result.transpose(0, 2, 1, 3)
    return result.reshape(lay_dev, rows, 1, share * HD)


def solution(mesh):
    return jax.shard_map(
        body,
        mesh=mesh,
        in_specs=(
            P("lay", ("groups", "tok"), "head"),
            P("lay", ("groups", "tok"), "head"),
            P("lay", "groups", "head"),
            P(("groups", "tok"), None),
            P("groups"),
        ),
        out_specs=P("lay", "groups", "head", "tok"),
        check_vma=False,
    )
```

profile of v0, /device:TPU:0, one launch (start us, length us, event | category | flops | bytes accessed | tf_op | source)
XLA Modules:
  0.0 476.8 jit_solution(16566091933869575326)
XLA Ops:
  6.5 3.0 fusion.71
  9.6 2.6 fusion.9
  12.4 46.5 %all-reduce.18.cloned.1.call-done = (f32[512,256]{1,0:T(8,128)}, f32[256,256]{0,1:T(8,128)}) async-done(((f32[512,256]{1,0:T(8,128)}, f32[256,256]{0,1:T(8,128)}), (f32[512,256]{1,0:T(8,128)}, f32[256,256]{0,1:T(8,128)})) %all-reduce.18.cloned.1.call-update) | async-done | bytes 786448 | tf_op jit(solution)/shard_map/psum | solution.py:63
  59.0 1.1 copy.45
  60.2 11.7 %cholesky.172 = f32[128,128]{1,0:T(8,128)S(1)} custom-call(f32[128,128]{1,0:T(8,128)S(1)} %cholesky.270), custom_call_target="Cholesky" | custom-call | tf_op jit(solution)/shard_map/jit(cholesky)/cholesky | solution.py:64
  71.9 9.8 %custom-call.16 = f32[1,128,128]{1,2,0:T(8,128)S(1)} custom-call(f32[1,128,128]{2,1,0:T(8,128)S(1)} %get-tuple-element.288), custom_call_target="InvertDiagBlocksLowerTriangular" | custom-call | tf_op jit(solution)/shard_map/jit(cholesky)/cholesky | solution.py:64
  82.3 11.7 %cholesky.189 = f32[128,128]{1,0:T(8,128)S(1)} custom-call(f32[128,128]{1,0:T(8,128)S(1)} %convolution_subtract_fusion.6), custom_call_target="Cholesky" | custom-call | tf_op jit(solution)/shard_map/jit(cholesky)/cholesky | solution.py:64
  96.2 4.5 while.28
  97.1 1.4 bitcast_dynamic-update-slice_fusion.6
  99.2 1.4 bitcast_dynamic-update-slice_fusion.6
  100.7 19.7 %custom-call.17 = f32[2,128,128]{1,2,0:T(8,128)S(1)} custom-call(f32[2,128,128]{2,1,0:T(8,128)S(1)} %get-tuple-element.212), custom_call_target="InvertDiagBlocksLowerTriangular" | custom-call | tf_op jit(solution)/shard_map/triangular_solve/custom-call.0 | solution.py:32
  121.8 1.9 convolution_bitcast_fusion.3
  123.8 32.6 %all-reduce.10.cloned.1.call-done = f32[512,256]{0,1:T(8,128)} async-done(((f32[512,256]{0,1:T(8,128)}), f32[512,256]{0,1:T(8,128)}) %all-reduce.10.cloned.1.call-update) | async-done | bytes 524304 | tf_op jit(solution)/shard_map/psum | solution.py:41
  156.4 3.0 convolution_bitcast_fusion.2
  159.3 1.3 fusion.72
  161.1 43.7 %all-reduce.16.cloned.1.call-done = (f32[512,256]{0,1:T(8,128)}, f32[256,256]{0,1:T(8,128)}) async-done(((f32[512,256]{0,1:T(8,128)}, f32[256,256]{0,1:T(8,128)}), (f32[512,256]{0,1:T(8,128)}, f32[256,256]{0,1:T(8,128)})) %all-reduce.16.cloned.1.call-update) | async-done | bytes 786448 | tf_op jit(solution)/shard_map/psum | solution.py:63
  204.8 1.1 copy.47
  206.0 11.7 %cholesky.206 = f32[128,128]{1,0:T(8,128)S(1)} custom-call(f32[128,128]{1,0:T(8,128)S(1)} %cholesky.273), custom_call_target="Cholesky" | custom-call | tf_op jit(solution)/shard_map/jit(cholesky)/cholesky | solution.py:64
  217.8 9.8 %custom-call.18 = f32[1,128,128]{1,2,0:T(8,128)S(1)} custom-call(f32[1,128,128]{2,1,0:T(8,128)S(1)} %get-tuple-element.284), custom_call_target="InvertDiagBlocksLowerTriangular" | custom-call | tf_op jit(solution)/shard_map/jit(cholesky)/cholesky | solution.py:64
  228.1 11.7 %cholesky.223 = f32[128,128]{1,0:T(8,128)S(1)} custom-call(f32[128,128]{1,0:T(8,128)S(1)} %convolution_subtract_fusion.5), custom_call_target="Cholesky" | custom-call | tf_op jit(solution)/shard_map/jit(cholesky)/cholesky | solution.py:64
  242.6 16.1 %while.29 = (s32[]{:T(128)}, f32[256,256]{1,0:T(8,128)S(1)}, s32[2,2]{1,0:T(2,128)S(1)}, f32[2,128,128]{2,1,0:T(8,128)S(1)}, s32[]{:T(128)}) while((s32[]{:T(128)}, f32[256,256]{1,0:T(8,128)S(1)}, s32[2,2]{1,0:T(2,128)S(1)}, f32[2,128,128]{2,1,0:T(8,128)S(1)}, s32[]{:T(128)}) %tuple.129), condition=%wide.while_cond.clone, body=%wide.while_body.clone.sunk | while | flops 2 | bytes 131181 | solution.py:32
  255.1 1.4 bitcast_dynamic-update-slice_fusion.7
  257.3 1.4 bitcast_dynamic-update-slice_fusion.7
  258.7 19.7 %custom-call.19 = f32[2,128,128]{1,2,0:T(8,128)S(1)} custom-call(f32[2,128,128]{2,1,0:T(8,128)S(1)} %get-tuple-element.213), custom_call_target="InvertDiagBlocksLowerTriangular" | custom-call | tf_op jit(solution)/shard_map/triangular_solve/custom-call.0 | solution.py:32
  279.7 1.9 convolution_bitcast_fusion.1
  281.6 32.6 %all-reduce.12.cloned.1.call-done = f32[512,256]{0,1:T(8,128)} async-done(((f32[512,256]{0,1:T(8,128)}), f32[512,256]{0,1:T(8,128)}) %all-reduce.12.cloned.1.call-update) | async-done | bytes 524304 | tf_op jit(solution)/shard_map/psum | solution.py:41
  314.2 3.0 convolution_bitcast_fusion
  317.2 1.3 fusion.73
  321.1 1.6 reshape.164
  322.7 39.9 %all-reduce.14.cloned.1.call-done = (f32[512,256]{0,1:T(8,128)}, f32[256,256]{0,1:T(8,128)}) async-done(((f32[512,256]{0,1:T(8,128)}, f32[256,256]{0,1:T(8,128)}), (f32[512,256]{0,1:T(8,128)}, f32[256,256]{0,1:T(8,128)})) %all-reduce.14.cloned.1.call-update) | async-done | bytes 786448 | tf_op jit(solution)/shard_map/psum | solution.py:63
  362.6 1.1 copy.50
  363.8 11.7 %cholesky.240 = f32[128,128]{1,0:T(8,128)S(1)} custom-call(f32[128,128]{1,0:T(8,128)S(1)} %cholesky.276), custom_call_target="Cholesky" | custom-call | tf_op jit(solution)/shard_map/jit(cholesky)/cholesky | solution.py:64
  375.6 9.8 %custom-call.20 = f32[1,128,128]{1,2,0:T(8,128)S(1)} custom-call(f32[1,128,128]{2,1,0:T(8,128)S(1)} %get-tuple-element.280), custom_call_target="InvertDiagBlocksLowerTriangular" | custom-call | tf_op jit(solution)/shard_map/jit(cholesky)/cholesky | solution.py:64
  385.9 11.7 %cholesky.257 = f32[128,128]{1,0:T(8,128)S(1)} custom-call(f32[128,128]{1,0:T(8,128)S(1)} %convolution_subtract_fusion.4), custom_call_target="Cholesky" | custom-call | tf_op jit(solution)/shard_map/jit(cholesky)/cholesky | solution.py:64
  400.5 4.5 while.30
  401.3 1.4 bitcast_dynamic-update-slice_fusion.8
  403.5 1.4 bitcast_dynamic-update-slice_fusion.8
  404.9 19.7 %custom-call.21 = f32[2,128,128]{1,2,0:T(8,128)S(1)} custom-call(f32[2,128,128]{2,1,0:T(8,128)S(1)} %get-tuple-element.214), custom_call_target="InvertDiagBlocksLowerTriangular" | custom-call | tf_op jit(solution)/shard_map/triangular_solve/custom-call.0 | solution.py:32
  426.6 1.1 fusion.61
  429.2 1.7 convolution_multiply_fusion
  430.9 1.9 select_reduce_fusion
  432.8 2.6 fusion.11
  436.0 13.2 %all_gather.10 = f32[4,1,32,16]{2,3,1,0:T(8,128)S(1)} all-gather(f32[1,1,32,16]{2,3,1,0:T(8,128)S(1)} %copy.57), channel_id=1, replica_groups=mesh['groups'=2,'tok'=4,'lay'=2,'head'=2] {'tok'}, dimensions={0}, use_global_device_ids=true | all-gather | bytes 10240 | tf_op jit(solution)/shard_map/all_gather | solution.py:15
  449.2 13.3 %all_gather.9 = f32[4,1,32,16]{2,3,1,0:T(8,128)S(1)} all-gather(f32[1,1,32,16]{2,3,1,0:T(8,128)S(1)} %copy.56), channel_id=1, replica_groups=mesh['groups'=2,'tok'=4,'lay'=2,'head'=2] {'tok'}, dimensions={0}, use_global_device_ids=true | all-gather | bytes 10240 | tf_op jit(solution)/shard_map/all_gather | solution.py:15
  464.5 4.3 while.27
  464.7 1.2 fusion.107
  466.2 1.2 fusion.107
  467.6 1.2 fusion.107
  (138 shorter events, 22.8 us)
Async XLA Ops:
  6.5 3.0 copy-start
  6.5 3.0 copy-start.2
  6.5 52.4 %all-reduce.18.cloned.1.call-start = ((), (), s32[]{:S(2)}) async-start(), calls=%async_computation.5 | async-start | bytes 1572864 | tf_op jit(solution)/shard_map/psum | solution.py:63
  12.2 144.2 %all-reduce.10.cloned.1.call-start = ((), (), s32[]{:S(2)}) async-start(), calls=%async_computation | async-start | bytes 1048576 | tf_op jit(solution)/shard_map/psum | solution.py:41
  59.0 1.2 copy-start.6
  96.1 24.3 %copy-start.13 = (f32[512,256]{1,0:T(8,128)S(1)}, f32[512,256]{1,0:T(8,128)}, u32[]{:S(2)}) copy-start(f32[512,256]{1,0:T(8,128)} %get-tuple-element.265) | copy-start | bytes 1572868
  123.7 81.1 %all-reduce.16.cloned.1.call-start = ((), (), s32[]{:S(2)}) async-start(), calls=%async_computation.4 | async-start | bytes 1572864 | tf_op jit(solution)/shard_map/psum | solution.py:63
  156.4 3.0 copy-start.3
  160.7 153.5 %all-reduce.12.cloned.1.call-start = ((), (), s32[]{:S(2)}) async-start(), calls=%async_computation.1 | async-start | bytes 1048576 | tf_op jit(solution)/shard_map/psum | solution.py:41
  204.8 1.2 copy-start.7
  242.6 35.8 %copy-start.14 = (f32[512,256]{0,1:T(8,128)S(1)}, f32[512,256]{0,1:T(8,128)}, u32[]{:S(2)}) copy-start(f32[512,256]{0,1:T(8,128)} %get-tuple-element.263) | copy-start | bytes 1572868
  281.5 81.0 %all-reduce.14.cloned.1.call-start = ((), (), s32[]{:S(2)}) async-start(), calls=%async_computation.3 | async-start | bytes 1572864 | tf_op jit(solution)/shard_map/psum | solution.py:63
  314.2 3.0 copy-start.1
  318.5 0.9 copy-start.15
  318.5 145.0 %all-gather.2.cloned.1.call-start = ((), (), s32[]{:S(2)}) async-start(), calls=%async_computation.2 | async-start | bytes 1310720 | tf_op jit(solution)/shard_map/all_gather | solution.py:15
  320.2 0.7 copy-start.16
  362.6 1.2 copy-start.4
  363.8 11.7 %copy-start.8 = (f32[256,256]{1,0:T(8,128)}, f32[256,256]{1,0:T(8,128)S(1)}, u32[]{:S(2)}) copy-start(f32[256,256]{1,0:T(8,128)S(1)} %fusion.34) | copy-start | bytes 786436
  375.6 9.8 %copy-start.9 = (f32[256,256]{1,0:T(8,128)S(1)}, f32[256,256]{1,0:T(8,128)}, u32[]{:S(2)}) copy-start(f32[256,256]{1,0:T(8,128)} %copy-done.8) | copy-start | bytes 786436
  424.6 0.6 copy-start.10
  425.7 0.9 copy-start.11
  425.7 2.0 copy-start.12
  429.2 1.7 copy-start.5
Sparse Core Ops, SparseCore 0:
  12.3 46.5 all-reduce.17
  123.8 32.5 all-reduce.9
  160.8 43.8 all-reduce.15
  281.7 32.4 all-reduce.11
  318.6 43.8 all-reduce.13
  435.6 27.8 all-gather.1
where the time goes:
time: 480 us; the launch traced here: 477 us
  waiting for transfers between devices  196 us (41%)
  other arithmetic  167 us (35%)
  matrix products  31.4 us (7%)
  blocking collectives  26.5 us (6%)
  local copies, waits for them, and re-layouts  24 us (5%)
  between operations  18.3 us (4%)
  loops' own time  12.5 us (3%)
    psum x3, waiting for transfers between devices, finish(): gram, proj = lax.psum((gram_of(block), project(keys, block)), 'tok')  130 us
    another operation x20, other arithmetic, finish(): lower = jnp.linalg.cholesky(gram)  103 us
    psum x2, waiting for transfers between devices, mix_block(): return lax.psum(partial_block, ('lay', 'head'))  65.2 us
    another operation x8, other arithmetic, right_solve(): lax.linalg.triangular_solve(lower, matrix, left_side=False, lower=True, t...  59.2 us
    all_gather x2, blocking collectives, joined(): gathered = jax.tree.map(lambda a: lax.all_gather(a, axis), part)  26.5 us
    another operation x22, local copies, waits for them, and re-layouts, right_solve(): lax.linalg.triangular_solve(lower, matrix, left_side=False, lower=True, t...  12.7 us
    another operation x3, loops' own time, right_solve(): lax.linalg.triangular_solve(lower, matrix, left_side=False, lower=True, t...  12.4 us
  transfers between devices with their start and end apart: 6, of which 6 were waited for; matrix products, arithmetic and copies ran while one was open for 1% of the time, Pallas kernels for 0%

commit v1 on v0

--- a/solution.py
+++ b/solution.py
@@ -1,14 +1,25 @@
+import functools
 import math
 import jax
 import jax.numpy as jnp
 from jax import lax
 from jax.sharding import PartitionSpec as P
+from jax.lax import psum
 
 KVH = 8
 HD = 128
 QH = 64
 ITERS = 2
 NEG = -1e30
+
+
+def create_points_here(q_in, shard_axis, group_axis):
+    for s in (shard_axis, group_axis):
+        q_in = psum(q_in, s)
+    return q_in
+
+
+bind_tables = functools.partial(create_points_here, shard_axis="head", group_axis="lay")
 
 
 def joined(part, axis, combine):
@@ -38,7 +49,7 @@
 
 def mix_block(keys, coef):
     partial_block = jnp.einsum("lsc,lcr->sr", keys, coef, precision=lax.Precision.HIGHEST)
-    return lax.psum(partial_block, ("lay", "head"))
+    return bind_tables(partial_block)
 
 
 def combine(first, second):

time: 480 us -> 516 us (1.075)
  waiting for transfers between devices: 196 us -> 232 us
    psum x2 -> x4, waiting for transfers between devices: 65.2 us -> 100 us  [create_points_here(): q_in = psum(q_in, s)]
  transfers between devices with their start and end apart: 6 -> 8, of which waited for: 6 -> 8; matrix products, arithmetic and copies ran while one was open for 1% -> 1% of each run, Pallas kernels for 0% -> 0%
where the time goes in v1:
time: 516 us; the launch traced here: 512 us
  waiting for transfers between devices  232 us (45%)
  other arithmetic  167 us (32%)
  matrix products  31.4 us (6%)
  blocking collectives  26.5 us (5%)
  local copies, waits for them, and re-layouts  24 us (5%)
  between operations  18.3 us (4%)
  loops' own time  12.6 us (2%)
    psum x3, waiting for transfers between devices, finish(): gram, proj = lax.psum((gram_of(block), project(keys, block)), 'tok')  130 us
    another operation x20, other arithmetic, finish(): lower = jnp.linalg.cholesky(gram)  103 us
    psum x4, waiting for transfers between devices, create_points_here(): q_in = psum(q_in, s)  100 us
    another operation x8, other arithmetic, right_solve(): lax.linalg.triangular_solve(lower, matrix, left_side=False, lower=True, t...  59.2 us
    all_gather x2, blocking collectives, joined(): gathered = jax.tree.map(lambda a: lax.all_gather(a, axis), part)  26.5 us
    another operation x22, local copies, waits for them, and re-layouts, right_solve(): lax.linalg.triangular_solve(lower, matrix, left_side=False, lower=True, t...  12.7 us
    another operation x3, loops' own time, right_solve(): lax.linalg.triangular_solve(lower, matrix, left_side=False, lower=True, t...  12.4 us
  transfers between devices with their start and end apart: 8, of which 8 were waited for; matrix products, arithmetic and copies ran while one was open for 1% of the time, Pallas kernels for 0%

profile of v1, /device:TPU:0, one launch (start us, length us, event | category | flops | bytes accessed | tf_op | source)
XLA Modules:
  0.0 512.1 jit_solution(1451805544435260492)
XLA Ops:
  6.5 3.0 fusion.71
  9.6 2.6 fusion.9
  12.4 46.5 %all-reduce.24.cloned.1.call-done = (f32[512,256]{1,0:T(8,128)}, f32[256,256]{0,1:T(8,128)}) async-done(((f32[512,256]{1,0:T(8,128)}, f32[256,256]{0,1:T(8,128)}), (f32[512,256]{1,0:T(8,128)}, f32[256,256]{0,1:T(8,128)})) %all-reduce.24.cloned.1.call-update) | async-done | bytes 786448 | tf_op jit(solution)/shard_map/psum | solution.py:74
  59.0 1.1 copy.45
  60.2 11.7 %cholesky.172 = f32[128,128]{1,0:T(8,128)S(1)} custom-call(f32[128,128]{1,0:T(8,128)S(1)} %cholesky.270), custom_call_target="Cholesky" | custom-call | tf_op jit(solution)/shard_map/jit(cholesky)/cholesky | solution.py:75
  71.9 9.8 %custom-call.16 = f32[1,128,128]{1,2,0:T(8,128)S(1)} custom-call(f32[1,128,128]{2,1,0:T(8,128)S(1)} %get-tuple-element.288), custom_call_target="InvertDiagBlocksLowerTriangular" | custom-call | tf_op jit(solution)/shard_map/jit(cholesky)/cholesky | solution.py:75
  82.3 11.7 %cholesky.189 = f32[128,128]{1,0:T(8,128)S(1)} custom-call(f32[128,128]{1,0:T(8,128)S(1)} %convolution_subtract_fusion.6), custom_call_target="Cholesky" | custom-call | tf_op jit(solution)/shard_map/jit(cholesky)/cholesky | solution.py:75
  96.2 4.5 while.28
  97.1 1.4 bitcast_dynamic-update-slice_fusion.6
  99.2 1.4 bitcast_dynamic-update-slice_fusion.6
  100.7 19.7 %custom-call.17 = f32[2,128,128]{1,2,0:T(8,128)S(1)} custom-call(f32[2,128,128]{2,1,0:T(8,128)S(1)} %get-tuple-element.212), custom_call_target="InvertDiagBlocksLowerTriangular" | custom-call | tf_op jit(solution)/shard_map/triangular_solve/custom-call.0 | solution.py:43
  121.8 1.9 convolution_bitcast_fusion.3
  123.8 18.2 %all-reduce.12.cloned.1.call-done = f32[512,256]{0,1:T(8,128)} async-done(((f32[512,256]{0,1:T(8,128)}), f32[512,256]{0,1:T(8,128)}) %all-reduce.12.cloned.1.call-update) | async-done | bytes 524304 | tf_op jit(solution)/shard_map/psum | solution.py:18
  142.0 32.1 %all-reduce.14.cloned.1.call-done = f32[512,256]{0,1:T(8,128)} async-done(((f32[512,256]{0,1:T(8,128)}), f32[512,256]{0,1:T(8,128)}) %all-reduce.14.cloned.1.call-update) | async-done | bytes 524304 | tf_op jit(solution)/shard_map/psum | solution.py:18
  174.1 3.0 convolution_bitcast_fusion.2
  177.1 1.3 fusion.72
  178.8 43.7 %all-reduce.22.cloned.1.call-done = (f32[512,256]{0,1:T(8,128)}, f32[256,256]{0,1:T(8,128)}) async-done(((f32[512,256]{0,1:T(8,128)}, f32[256,256]{0,1:T(8,128)}), (f32[512,256]{0,1:T(8,128)}, f32[256,256]{0,1:T(8,128)})) %all-reduce.22.cloned.1.call-update) | async-done | bytes 786448 | tf_op jit(solution)/shard_map/psum | solution.py:74
  222.5 1.1 copy.47
  223.7 11.7 %cholesky.206 = f32[128,128]{1,0:T(8,128)S(1)} custom-call(f32[128,128]{1,0:T(8,128)S(1)} %cholesky.273), custom_call_target="Cholesky" | custom-call | tf_op jit(solution)/shard_map/jit(cholesky)/cholesky | solution.py:75
  235.5 9.8 %custom-call.18 = f32[1,128,128]{1,2,0:T(8,128)S(1)} custom-call(f32[1,128,128]{2,1,0:T(8,128)S(1)} %get-tuple-element.284), custom_call_target="InvertDiagBlocksLowerTriangular" | custom-call | tf_op jit(solution)/shard_map/jit(cholesky)/cholesky | solution.py:75
  245.8 11.7 %cholesky.223 = f32[128,128]{1,0:T(8,128)S(1)} custom-call(f32[128,128]{1,0:T(8,128)S(1)} %convolution_subtract_fusion.5), custom_call_target="Cholesky" | custom-call | tf_op jit(solution)/shard_map/jit(cholesky)/cholesky | solution.py:75
  260.4 16.1 %while.29 = (s32[]{:T(128)}, f32[256,256]{1,0:T(8,128)S(1)}, s32[2,2]{1,0:T(2,128)S(1)}, f32[2,128,128]{2,1,0:T(8,128)S(1)}, s32[]{:T(128)}) while((s32[]{:T(128)}, f32[256,256]{1,0:T(8,128)S(1)}, s32[2,2]{1,0:T(2,128)S(1)}, f32[2,128,128]{2,1,0:T(8,128)S(1)}, s32[]{:T(128)}) %tuple.133), condition=%wide.while_cond.clone, body=%wide.while_body.clone.sunk | while | flops 2 | bytes 131181 | solution.py:43
  272.9 1.4 bitcast_dynamic-update-slice_fusion.7
  275.0 1.4 bitcast_dynamic-update-slice_fusion.7
  276.5 19.7 %custom-call.19 = f32[2,128,128]{1,2,0:T(8,128)S(1)} custom-call(f32[2,128,128]{2,1,0:T(8,128)S(1)} %get-tuple-element.213), custom_call_target="InvertDiagBlocksLowerTriangular" | custom-call | tf_op jit(solution)/shard_map/triangular_solve/custom-call.0 | solution.py:43
  297.4 1.9 convolution_bitcast_fusion.1
  299.4 18.2 %all-reduce.16.cloned.1.call-done = f32[512,256]{0,1:T(8,128)} async-done(((f32[512,256]{0,1:T(8,128)}), f32[512,256]{0,1:T(8,128)}) %all-reduce.16.cloned.1.call-update) | async-done | bytes 524304 | tf_op jit(solution)/shard_map/psum | solution.py:18
  317.6 32.0 %all-reduce.18.cloned.1.call-done = f32[512,256]{0,1:T(8,128)} async-done(((f32[512,256]{0,1:T(8,128)}), f32[512,256]{0,1:T(8,128)}) %all-reduce.18.cloned.1.call-update) | async-done | bytes 524304 | tf_op jit(solution)/shard_map/psum | solution.py:18
  349.6 3.0 convolution_bitcast_fusion
  352.5 1.3 fusion.73
  356.5 1.6 reshape.164
  358.0 39.9 %all-reduce.20.cloned.1.call-done = (f32[512,256]{0,1:T(8,128)}, f32[256,256]{0,1:T(8,128)}) async-done(((f32[512,256]{0,1:T(8,128)}, f32[256,256]{0,1:T(8,128)}), (f32[512,256]{0,1:T(8,128)}, f32[256,256]{0,1:T(8,128)})) %all-reduce.20.cloned.1.call-update) | async-done | bytes 786448 | tf_op jit(solution)/shard_map/psum | solution.py:74
  399.2 11.7 %cholesky.240 = f32[128,128]{1,0:T(8,128)S(1)} custom-call(f32[128,128]{1,0:T(8,128)S(1)} %cholesky.276), custom_call_target="Cholesky" | custom-call | tf_op jit(solution)/shard_map/jit(cholesky)/cholesky | solution.py:75
  411.0 9.8 %custom-call.20 = f32[1,128,128]{1,2,0:T(8,128)S(1)} custom-call(f32[1,128,128]{2,1,0:T(8,128)S(1)} %get-tuple-element.280), custom_call_target="InvertDiagBlocksLowerTriangular" | custom-call | tf_op jit(solution)/shard_map/jit(cholesky)/cholesky | solution.py:75
  421.3 11.7 %cholesky.257 = f32[128,128]{1,0:T(8,128)S(1)} custom-call(f32[128,128]{1,0:T(8,128)S(1)} %convolution_subtract_fusion.4), custom_call_target="Cholesky" | custom-call | tf_op jit(solution)/shard_map/jit(cholesky)/cholesky | solution.py:75
  435.8 4.5 while.30
  436.7 1.4 bitcast_dynamic-update-slice_fusion.8
  438.8 1.4 bitcast_dynamic-update-slice_fusion.8
  440.3 19.7 %custom-call.21 = f32[2,128,128]{1,2,0:T(8,128)S(1)} custom-call(f32[2,128,128]{2,1,0:T(8,128)S(1)} %get-tuple-element.214), custom_call_target="InvertDiagBlocksLowerTriangular" | custom-call | tf_op jit(solution)/shard_map/triangular_solve/custom-call.0 | solution.py:43
  464.6 1.7 convolution_multiply_fusion
  466.3 1.9 select_reduce_fusion
  468.2 2.6 fusion.11
  471.4 13.2 %all_gather.10 = f32[4,1,32,16]{2,3,1,0:T(8,128)S(1)} all-gather(f32[1,1,32,16]{2,3,1,0:T(8,128)S(1)} %copy.57), channel_id=1, replica_groups=mesh['groups'=2,'tok'=4,'lay'=2,'head'=2] {'tok'}, dimensions={0}, use_global_device_ids=true | all-gather | bytes 10240 | tf_op jit(solution)/shard_map/all_gather | solution.py:26
  484.5 13.3 %all_gather.9 = f32[4,1,32,16]{2,3,1,0:T(8,128)S(1)} all-gather(f32[1,1,32,16]{2,3,1,0:T(8,128)S(1)} %copy.56), channel_id=1, replica_groups=mesh['groups'=2,'tok'=4,'lay'=2,'head'=2] {'tok'}, dimensions={0}, use_global_device_ids=true | all-gather | bytes 10240 | tf_op jit(solution)/shard_map/all_gather | solution.py:26
  499.9 4.3 while.27
  500.1 1.2 fusion.107
  501.5 1.2 fusion.107
  503.0 1.2 fusion.107
  (144 shorter events, 25.1 us)
Async XLA Ops:
  6.5 3.0 copy-start
  6.5 3.0 copy-start.2
  6.5 52.4 %all-reduce.24.cloned.1.call-start = ((), (), s32[]{:S(2)}) async-start(), calls=%async_computation.7 | async-start | bytes 1572864 | tf_op jit(solution)/shard_map/psum | solution.py:74
  12.2 129.7 %all-reduce.12.cloned.1.call-start = ((), (), s32[]{:S(2)}) async-start(), calls=%async_computation | async-start | bytes 1048576 | tf_op jit(solution)/shard_map/psum | solution.py:18
  59.0 1.2 copy-start.6
  96.1 24.3 %copy-start.13 = (f32[512,256]{1,0:T(8,128)S(1)}, f32[512,256]{1,0:T(8,128)}, u32[]{:S(2)}) copy-start(f32[512,256]{1,0:T(8,128)} %get-tuple-element.265) | copy-start | bytes 1572868
  123.7 50.4 %all-reduce.14.cloned.1.call-start = ((), (), s32[]{:S(2)}) async-start(), calls=%async_computation.1 | async-start | bytes 1048576 | tf_op jit(solution)/shard_map/psum | solution.py:18
  141.9 80.6 %all-reduce.22.cloned.1.call-start = ((), (), s32[]{:S(2)}) async-start(), calls=%async_computation.6 | async-start | bytes 1572864 | tf_op jit(solution)/shard_map/psum | solution.py:74
  174.1 3.0 copy-start.3
  178.4 139.1 %all-reduce.16.cloned.1.call-start = ((), (), s32[]{:S(2)}) async-start(), calls=%async_computation.2 | async-start | bytes 1048576 | tf_op jit(solution)/shard_map/psum | solution.py:18
  222.5 1.2 copy-start.7
  260.3 35.9 %copy-start.14 = (f32[512,256]{0,1:T(8,128)S(1)}, f32[512,256]{0,1:T(8,128)}, u32[]{:S(2)}) copy-start(f32[512,256]{0,1:T(8,128)} %get-tuple-element.263) | copy-start | bytes 1572868
  299.3 50.3 %all-reduce.18.cloned.1.call-start = ((), (), s32[]{:S(2)}) async-start(), calls=%async_computation.3 | async-start | bytes 1048576 | tf_op jit(solution)/shard_map/psum | solution.py:18
  317.5 80.4 %all-reduce.20.cloned.1.call-start = ((), (), s32[]{:S(2)}) async-start(), calls=%async_computation.5 | async-start | bytes 1572864 | tf_op jit(solution)/shard_map/psum | solution.py:74
  349.6 3.0 copy-start.1
  353.8 0.9 copy-start.15
  353.9 145.0 %all-gather.2.cloned.1.call-start = ((), (), s32[]{:S(2)}) async-start(), calls=%async_computation.4 | async-start | bytes 1310720 | tf_op jit(solution)/shard_map/all_gather | solution.py:26
  355.5 0.7 copy-start.16
  397.9 1.2 copy-start.4
  399.1 11.7 %copy-start.8 = (f32[256,256]{1,0:T(8,128)}, f32[256,256]{1,0:T(8,128)S(1)}, u32[]{:S(2)}) copy-start(f32[256,256]{1,0:T(8,128)S(1)} %fusion.34) | copy-start | bytes 786436
  410.9 9.8 %copy-start.9 = (f32[256,256]{1,0:T(8,128)S(1)}, f32[256,256]{1,0:T(8,128)}, u32[]{:S(2)}) copy-start(f32[256,256]{1,0:T(8,128)} %copy-done.8) | copy-start | bytes 786436
  460.0 0.6 copy-start.10
  461.1 0.9 copy-start.11
  461.1 2.0 copy-start.12
  464.6 1.7 copy-start.5
Sparse Core Ops, SparseCore 0:
  12.3 46.5 all-reduce.23
  123.8 18.0 all-reduce.11
  144.3 29.7 all-reduce.13
  178.5 43.8 all-reduce.21
  299.4 18.0 all-reduce.15
  319.8 29.7 all-reduce.17
  354.0 43.8 all-reduce.19
  471.0 27.8 all-gather.1
